TPU v7x, 32 devices: a whole 2x2x4 slice. The times are simulated.
32 devices in a mesh: sx: 8 (over y, x, core), sy: 4 (over z).
Axes of the slice: x: 2, y: 2, z: 4, core: 2. Of those that a mesh axis runs over, the one named last changes fastest.
Arguments:
- adjoint_loads: float32 [8, 8, 2, 288, 128], P('sx', 'sy'), may hold values from -6 to 6
- dual_taut: bfloat16 [8, 8, 1152, 1152], P('sx', 'sy'), may hold values from -1 to 2
- dual_wrinkle: bfloat16 [8, 8, 1152, 1152], P('sx', 'sy'), may hold values from -1 to 2
- dirichlet_taut: bfloat16 [8, 8, 1152, 1152], P('sx', 'sy'), may hold values from -1 to 2
- dirichlet_wrinkle: bfloat16 [8, 8, 1152, 1152], P('sx', 'sy'), may hold values from -1 to 2
- coupling: bfloat16 [8, 8, 12, 1152], P('sx', 'sy'), may hold values from -0.25 to 0.25
- coarse_inverse: bfloat16 [256, 256], P('sx', 'sy'), may hold values from -1 to 2
- wrinkled: int32 [8, 8], P('sx', 'sy'), may hold values 0 or 1
- edge_lengths: int32 [8, 8, 2], P('sx', 'sy'), may hold values from 144 to 288
- corner_map: int32 [8, 8, 12], P('sx', 'sy'), may hold values from 0 to 255, as said below
Outputs:
- multipliers: float32 [8, 8, 2, 288, 128], P('sx', 'sy')
- preconditioned: float32 [8, 8, 2, 288, 128], P('sx', 'sy')
Inputs may be any that keep to these rules, and one draw needn't show every extreme that they name: `corner_map`: each subdomain names 12 distinct coarse indices, three for each of its four grid corners; subdomains that meet at a grid corner name the same three indices for it; distinct grid corners name distinct indices.
All inputs are finite; a program needn't handle non-finite values. No bound on the sum of `wrinkled` on one device may be relied on, other than what follows from the above.
Results may differ from a plain program's by a relative error of at most 0.012.
Values may be sent and summed in bfloat16 or wider, within the bound.
A program may use at most 64 MiB of HBM per device.

v0:
```python
import jax
import jax.numpy as jnp
from jax import lax
from jax.sharding import PartitionSpec as P

EDGE = 288
CORNERS = 12
ITERS = 2
step_sizes = (0.55, 0.75)
momenta = (0.0, 0.15)


def from_behind(shard, axis, by):
    peers = lax.axis_size(axis)
    pairs = [(i, i + by) for i in range(peers) if 0 <= i + by < peers]
    return lax.ppermute(shard, axis, pairs)


def edge_mask(edge_lengths):
    per_row = edge_lengths.shape[1]
    shape_all = (1, per_row, 2, EDGE)
    positions = lax.broadcasted_iota(jnp.int32, shape_all, 3)
    inside = positions < edge_lengths[:, :, :, None]
    columns = lax.axis_index("sy") * per_row + lax.broadcasted_iota(jnp.int32, shape_all, 1)
    edge_kind = lax.broadcasted_iota(jnp.int32, shape_all, 2)
    exists = jnp.where(
        edge_kind == 0,
        columns < per_row * lax.axis_size("sy") - 1,
        lax.axis_index("sx") < lax.axis_size("sx") - 1,
    )
    return (inside & exists).astype(jnp.float32)[..., None]


def spread(edges):
    east_edge = edges[:, :, 0]
    south_edge = edges[:, :, 1]
    from_left = from_behind(east_edge[:, -1:], "sy", 1)
    west_edge = jnp.concatenate([from_left, east_edge[:, :-1]], axis=1)
    north_edge = from_behind(south_edge, "sx", 1)
    return jnp.concatenate([east_edge, south_edge, -west_edge, -north_edge], axis=2)


def collect(local_part):
    west_part = local_part[:, :, 2 * EDGE : 3 * EDGE]
    from_right = from_behind(west_part[:, :1], "sy", -1)
    right_west = jnp.concatenate([west_part[:, 1:], from_right], axis=1)
    down_north = from_behind(local_part[:, :, 3 * EDGE :], "sx", -1)
    return jnp.stack(
        [local_part[:, :, :EDGE] - right_west, local_part[:, :, EDGE : 2 * EDGE] - down_north],
        axis=2,
    )


def paired(taut, wrinkle, wrinkled, vectors):
    base_part = jnp.einsum("rsij,rsjl->rsil", taut, vectors, preferred_element_type=jnp.float32)
    extra_part = jnp.einsum("rsij,rsjl->rsil", wrinkle, vectors, preferred_element_type=jnp.float32)
    return base_part + wrinkled.astype(jnp.float32)[:, :, None, None] * extra_part


def coarse_term(coupling, corner_map, coarse_inverse, vectors):
    col_count = coarse_inverse.shape[1]
    coarse_order = col_count * lax.axis_size("sy")
    corner_terms = jnp.einsum(
        "rskj,rsjl->rskl", coupling, vectors, preferred_element_type=jnp.float32
    )
    corner_terms = corner_terms.reshape(-1, corner_terms.shape[-1])
    corner_index = corner_map.reshape(-1)
    selector = corner_index[:, None] == lax.broadcasted_iota(
        jnp.int32, (corner_index.shape[0], coarse_order), 1
    )
    selector_float = selector.astype(jnp.float32)
    placed = jnp.einsum("kc,kl->cl", selector_float, corner_terms, precision=lax.Precision.HIGHEST)
    totals = lax.psum(placed, ("sx", "sy"))
    column_part = lax.dynamic_slice_in_dim(totals, lax.axis_index("sy") * col_count, col_count, 0)
    row_part = jnp.dot(
        coarse_inverse, column_part.astype(jnp.bfloat16), preferred_element_type=jnp.float32
    )
    solved = lax.psum(row_part, "sy").astype(jnp.bfloat16)
    selector_half = selector.astype(jnp.bfloat16)
    selected = jnp.dot(
        selector_half,
        lax.all_gather(solved, "sx", axis=0, tiled=True),
        preferred_element_type=jnp.float32,
    )
    selected = selected.astype(jnp.bfloat16).reshape(
        vectors.shape[0], vectors.shape[1], CORNERS, -1
    )
    return jnp.einsum("rskj,rskl->rsjl", coupling, selected, preferred_element_type=jnp.float32)


def local(
    adjoint_loads,
    dual_taut,
    dual_wrinkle,
    dirichlet_taut,
    dirichlet_wrinkle,
    coupling,
    coarse_inverse,
    wrinkled,
    edge_lengths,
    corner_map,
):
    masking = edge_mask(edge_lengths)
    loads = adjoint_loads * masking

    def precondition(incoming):
        vectors = spread((0.5 * incoming).astype(jnp.bfloat16))
        return 0.5 * collect(paired(dirichlet_taut, dirichlet_wrinkle, wrinkled, vectors)) * masking

    multipliers = jnp.zeros_like(loads)
    direction = jnp.zeros_like(loads)
    residual = loads
    for number in range(ITERS):
        direction = precondition(residual) + momenta[number] * direction
        multipliers = multipliers + step_sizes[number] * direction
        dual_vectors = spread(multipliers.astype(jnp.bfloat16))
        local_part = paired(dual_taut, dual_wrinkle, wrinkled, dual_vectors)
        local_part = local_part + coarse_term(coupling, corner_map, coarse_inverse, dual_vectors)
        residual = loads - collect(local_part) * masking
    return (multipliers, precondition(residual))


def solution(mesh):
    placed = (
        P("sx", "sy", None, None, None),
        P("sx", "sy", None, None),
        P("sx", "sy", None, None),
        P("sx", "sy", None, None),
        P("sx", "sy", None, None),
        P("sx", "sy", None, None),
        P("sx", "sy"),
        P("sx", "sy"),
        P("sx", "sy", None),
        P("sx", "sy", None),
    )
    return jax.shard_map(
        local,
        mesh=mesh,
        in_specs=placed,
        out_specs=(P("sx", "sy", None, None, None), P("sx", "sy", None, None, None)),
        check_vma=False,
    )
```

profile of v0, /device:TPU:1, one launch (start us, length us, event | category | flops | bytes accessed | tf_op | source)
XLA Modules:
  0.0 320.2 jit_solution(4290553914124060883)
XLA Ops:
  0.7 0.8 copy.32
  1.4 1.3 copy.33
  3.0 4.0 %collective-permute-start = (bf16[1,1,288,128]{2,3,1,0:T(8,128)(2,1)S(1)}, bf16[1,1,288,128]{2,3,1,0:T(8,128)(2,1)S(1)}, u32[]{:S(2)}, u32[]{:S(2)}) collective-permute-start(bf16[1,1,288,128]{2,3,1,0:T(8,128)(2,1)S(1)} %get-tuple-element.48), channel_id=1, source_target_pairs={{0,1},{1,2},{2,3},{4,5},{5,6},{6,7},{8,9},{9,10},{10,11},{12,13},{... | collective-permute-start | bytes 221192 | tf_op jit(solution)/shard_map/ppermute | solution.py:16
  7.0 4.0 %collective-permute-start.1 = (bf16[1,2,288,128]{2,3,1,0:T(8,128)(2,1)S(1)}, bf16[1,2,288,128]{2,3,1,0:T(8,128)(2,1)S(1)}, u32[]{:S(2)}, u32[]{:S(2)}) collective-permute-start(bf16[1,2,288,128]{2,3,1,0:T(8,128)(2,1)S(1)} %get-tuple-element.38), channel_id=1, source_target_pairs={{0,4},{4,8},{8,12},{12,16},{16,20},{20,24},{24,28},{1,5},{5,9},{9,... | collective-permute-start | bytes 442376 | tf_op jit(solution)/shard_map/ppermute | solution.py:16
  11.1 2.5 collective-permute-done.1
  13.6 0.6 concatenate.138
  14.2 4.3 %fusion.29 = f32[2,128,1152]{2,1,0:T(8,128)S(1)} fusion(bf16[1,2,1152,1152]{3,2,1,0:T(8,128)(2,1)} %param.14, bf16[1,2,1152,128]{2,3,1,0:T(8,128)(2,1)S(1)} %concatenate.138, f32[2]{0:T(128)S(1)} %convert_bitcast_fusion), kind=kOutput, calls=%fused_computation.23 | convolution fusion | flops 679772160 | bytes 7077896 | tf_op jit(solution)/shard_map/rsij,rsjl->rsil/dot_general | solution.py:56
  18.6 1.7 fusion.68
  20.5 1.3 collective-permute-start.2
  21.8 5.1 %collective-permute-done.2 = f32[1,1,288,128]{2,3,1,0:T(8,128)S(1)} collective-permute-done((f32[1,1,288,128]{2,3,1,0:T(8,128)S(1)}, f32[1,1,288,128]{2,3,1,0:T(8,128)S(1)}, u32[]{:S(2)}, u32[]{:S(2)}) %collective-permute-start.2) | collective-permute-done | bytes 147488 | tf_op jit(solution)/shard_map/ppermute | solution.py:16
  27.1 1.9 collective-permute-start.3
  29.1 9.2 %collective-permute-done.3 = f32[1,2,288,128]{2,3,1,0:T(8,128)S(1)} collective-permute-done((f32[1,2,288,128]{2,3,1,0:T(8,128)S(1)}, f32[1,2,288,128]{2,3,1,0:T(8,128)S(1)}, u32[]{:S(2)}, u32[]{:S(2)}) %collective-permute-start.3) | collective-permute-done | bytes 294944 | tf_op jit(solution)/shard_map/ppermute | solution.py:16
  38.7 0.7 fusion.127
  39.3 3.2 collective-permute-start.4
  42.5 2.0 collective-permute-start.5
  44.6 0.8 eq.23
  45.3 0.7 maximum_negate_fusion.1
  46.0 1.1 collective-permute-done.5
  47.2 0.7 neg.73
  47.9 1.4 concatenate.141
  50.0 41.2 %all-reduce.2 = bf16[256,128]{1,0:T(8,128)(2,1)S(1)} all-reduce(f32[256,128]{1,0:T(8,128)S(1)} %fusion.109), channel_id=1, replica_groups=mesh['sx'=8,'sy'=4] {'sx','sy'}, use_global_device_ids=true, to_apply=%region_0.1 | all-reduce | flops 32768 | bytes 196608 | tf_op jit(solution)/shard_map/psum | solution.py:73
  91.2 0.8 convolution_bitcast_fusion.1
  92.1 13.2 %psum.29 = bf16[32,128]{1,0:T(8,128)(2,1)S(1)} all-reduce(f32[32,128]{1,0:T(8,128)S(1)} %convolution_bitcast_fusion.1), channel_id=1, replica_groups=mesh['sx'=8,'sy'=4] {'sy'}, use_global_device_ids=true, to_apply=%region_1.2 | all-reduce | flops 4096 | bytes 24576 | tf_op jit(solution)/shard_map/psum | solution.py:78
  105.2 15.1 %all_gather.6 = bf16[256,128]{1,0:T(8,128)(2,1)S(1)} all-gather(bf16[32,128]{1,0:T(8,128)(2,1)S(1)} %psum.29), channel_id=1, replica_groups=mesh['sx'=8,'sy'=4] {'sx'}, dimensions={0}, use_global_device_ids=true | all-gather | bytes 73728 | tf_op jit(solution)/shard_map/all_gather | solution.py:82
  120.9 4.4 %fusion.44 = f32[2,128,1152]{2,1,0:T(8,128)S(1)} fusion(bf16[1,2,1152,1152]{3,2,1,0:T(8,128)(2,1)} %param.12, bf16[1,2,1152,128]{2,3,1,0:T(8,128)(2,1)S(1)} %concatenate.141, f32[2]{0:T(128)S(1)} %convert_bitcast_fusion), kind=kOutput, calls=%fused_computation.28 | convolution fusion | flops 679772160 | bytes 7077896 | tf_op jit(solution)/shard_map/rsij,rsjl->rsil/dot_general | solution.py:56
  125.3 1.7 fusion.56
  127.2 1.3 collective-permute-start.6
  128.5 6.9 %collective-permute-done.6 = f32[1,1,288,128]{2,3,1,0:T(8,128)S(1)} collective-permute-done((f32[1,1,288,128]{2,3,1,0:T(8,128)S(1)}, f32[1,1,288,128]{2,3,1,0:T(8,128)S(1)}, u32[]{:S(2)}, u32[]{:S(2)}) %collective-permute-start.6) | collective-permute-done | bytes 147488 | tf_op jit(solution)/shard_map/ppermute | solution.py:16
  135.6 2.9 collective-permute-start.7
  138.5 7.0 %collective-permute-done.7 = f32[1,2,288,128]{2,3,1,0:T(8,128)S(1)} collective-permute-done((f32[1,2,288,128]{2,3,1,0:T(8,128)S(1)}, f32[1,2,288,128]{2,3,1,0:T(8,128)S(1)}, u32[]{:S(2)}, u32[]{:S(2)}) %collective-permute-start.7) | collective-permute-done | bytes 294944 | tf_op jit(solution)/shard_map/ppermute | solution.py:16
  145.9 1.5 collective-permute-start.8
  147.4 1.9 collective-permute-start.9
  149.4 2.5 collective-permute-done.9
  152.5 4.2 %fusion.32 = f32[2,128,1152]{2,1,0:T(8,128)S(1)} fusion(bf16[1,2,1152,1152]{3,2,1,0:T(8,128)(2,1)} %param.14, bf16[1,2,1152,128]{2,3,1,0:T(8,128)(2,1)S(1)} %concatenate.144, f32[2]{0:T(128)S(1)} %convert_bitcast_fusion), kind=kOutput, calls=%fused_computation.24 | convolution fusion | flops 679772160 | bytes 7077896 | tf_op jit(solution)/shard_map/rsij,rsjl->rsil/dot_general | solution.py:56
  156.7 4.2 %fusion.65 = f32[1,2,1152,128]{2,3,1,0:T(8,128)S(1)} fusion(f32[2,128,1152]{2,1,0:T(8,128)S(1)} %fusion.32, bf16[1,2,1152,1152]{3,2,1,0:T(8,128)(2,1)} %param.13, bf16[1,2,1152,128]{2,3,1,0:T(8,128)(2,1)S(1)} %concatenate.144), kind=kOutput, calls=%fused_computation.35 | convolution fusion | flops 679772160 | bytes 8257536 | tf_op jit(solution)/shard_map/rsij,rsjl->rsil/dot_general | solution.py:55
  161.1 1.3 collective-permute-start.10
  162.4 6.6 %collective-permute-done.10 = f32[1,1,288,128]{2,3,1,0:T(8,128)S(1)} collective-permute-done((f32[1,1,288,128]{2,3,1,0:T(8,128)S(1)}, f32[1,1,288,128]{2,3,1,0:T(8,128)S(1)}, u32[]{:S(2)}, u32[]{:S(2)}) %collective-permute-start.10) | collective-permute-done | bytes 147488 | tf_op jit(solution)/shard_map/ppermute | solution.py:16
  169.2 2.1 collective-permute-start.11
  171.3 8.1 %collective-permute-done.11 = f32[1,2,288,128]{2,3,1,0:T(8,128)S(1)} collective-permute-done((f32[1,2,288,128]{2,3,1,0:T(8,128)S(1)}, f32[1,2,288,128]{2,3,1,0:T(8,128)S(1)}, u32[]{:S(2)}, u32[]{:S(2)}) %collective-permute-start.11) | collective-permute-done | bytes 294944 | tf_op jit(solution)/shard_map/ppermute | solution.py:16
  179.6 1.1 fusion.117
  180.8 2.5 collective-permute-start.12
  183.4 1.9 collective-permute-start.13
  185.4 2.5 collective-permute-done.13
  187.9 0.6 concatenate.147
  188.8 4.2 %fusion.47 = f32[2,128,1152]{2,1,0:T(8,128)S(1)} fusion(bf16[1,2,1152,1152]{3,2,1,0:T(8,128)(2,1)} %param.12, bf16[1,2,1152,128]{2,3,1,0:T(8,128)(2,1)S(1)} %concatenate.147, f32[2]{0:T(128)S(1)} %convert_bitcast_fusion), kind=kOutput, calls=%fused_computation.29 | convolution fusion | flops 679772160 | bytes 7077896 | tf_op jit(solution)/shard_map/rsij,rsjl->rsil/dot_general | solution.py:56
  193.4 39.6 %all-reduce.3 = bf16[256,128]{1,0:T(8,128)(2,1)S(1)} all-reduce(f32[256,128]{1,0:T(8,128)S(1)} %fusion.108), channel_id=1, replica_groups=mesh['sx'=8,'sy'=4] {'sx','sy'}, use_global_device_ids=true, to_apply=%region_2.3 | all-reduce | flops 32768 | bytes 196608 | tf_op jit(solution)/shard_map/psum | solution.py:73
  233.2 13.5 %psum.31 = bf16[32,128]{1,0:T(8,128)(2,1)S(1)} all-reduce(f32[32,128]{1,0:T(8,128)S(1)} %convolution_bitcast_fusion), channel_id=1, replica_groups=mesh['sx'=8,'sy'=4] {'sy'}, use_global_device_ids=true, to_apply=%region_3.4 | all-reduce | flops 4096 | bytes 24576 | tf_op jit(solution)/shard_map/psum | solution.py:78
  246.7 15.0 %all_gather.7 = bf16[256,128]{1,0:T(8,128)(2,1)S(1)} all-gather(bf16[32,128]{1,0:T(8,128)(2,1)S(1)} %psum.31), channel_id=1, replica_groups=mesh['sx'=8,'sy'=4] {'sx'}, dimensions={0}, use_global_device_ids=true | all-gather | bytes 73728 | tf_op jit(solution)/shard_map/all_gather | solution.py:82
  262.3 4.2 %fusion.59 = f32[1,2,1152,128]{2,3,1,0:T(8,128)S(1)} fusion(f32[2,128,1152]{2,1,0:T(8,128)S(1)} %fusion.102, f32[2,128,1152]{2,1,0:T(8,128)S(1)} %fusion.47, bf16[1,2,1152,1152]{3,2,1,0:T(8,128)(2,1)} %param.11, bf16[1,2,1152,128]{2,3,1,0:T(8,128)(2,1)S(1)} %concatenate.147), kind=kOutput, calls=%fused_computation.33 | convolution fusion | flops 680067072 | bytes 9437184 | tf_op jit(solution)/shard_map/rsij,rsjl->rsil/dot_general | solution.py:55
  266.7 1.3 collective-permute-start.14
  268.0 6.9 %collective-permute-done.14 = f32[1,1,288,128]{2,3,1,0:T(8,128)S(1)} collective-permute-done((f32[1,1,288,128]{2,3,1,0:T(8,128)S(1)}, f32[1,1,288,128]{2,3,1,0:T(8,128)S(1)}, u32[]{:S(2)}, u32[]{:S(2)}) %collective-permute-start.14) | collective-permute-done | bytes 147488 | tf_op jit(solution)/shard_map/ppermute | solution.py:16
  275.0 2.9 collective-permute-start.15
  278.0 7.0 %collective-permute-done.15 = f32[1,2,288,128]{2,3,1,0:T(8,128)S(1)} collective-permute-done((f32[1,2,288,128]{2,3,1,0:T(8,128)S(1)}, f32[1,2,288,128]{2,3,1,0:T(8,128)S(1)}, u32[]{:S(2)}, u32[]{:S(2)}) %collective-permute-start.15) | collective-permute-done | bytes 294944 | tf_op jit(solution)/shard_map/ppermute | solution.py:16
  285.4 1.5 collective-permute-start.16
  286.9 1.9 collective-permute-start.17
  288.9 2.5 collective-permute-done.17
  292.0 4.2 %fusion.35 = f32[2,128,1152]{2,1,0:T(8,128)S(1)} fusion(bf16[1,2,1152,1152]{3,2,1,0:T(8,128)(2,1)} %param.14, bf16[1,2,1152,128]{2,3,1,0:T(8,128)(2,1)S(1)} %concatenate.150, f32[2]{0:T(128)S(1)} %convert_bitcast_fusion), kind=kOutput, calls=%fused_computation.25 | convolution fusion | flops 679772160 | bytes 7077896 | tf_op jit(solution)/shard_map/rsij,rsjl->rsil/dot_general | solution.py:56
  296.2 4.2 %fusion.62 = f32[1,2,1152,128]{2,3,1,0:T(8,128)S(1)} fusion(f32[2,128,1152]{2,1,0:T(8,128)S(1)} %fusion.35, bf16[1,2,1152,1152]{3,2,1,0:T(8,128)(2,1)} %param.13, bf16[1,2,1152,128]{2,3,1,0:T(8,128)(2,1)S(1)} %concatenate.150), kind=kOutput, calls=%fused_computation.34 | convolution fusion | flops 679772160 | bytes 8257536 | tf_op jit(solution)/shard_map/rsij,rsjl->rsil/dot_general | solution.py:55
  300.6 1.4 collective-permute-start.18
  302.0 6.6 %collective-permute-done.18 = f32[1,1,288,128]{2,3,1,0:T(8,128)S(1)} collective-permute-done((f32[1,1,288,128]{2,3,1,0:T(8,128)S(1)}, f32[1,1,288,128]{2,3,1,0:T(8,128)S(1)}, u32[]{:S(2)}, u32[]{:S(2)}) %collective-permute-start.18) | collective-permute-done | bytes 147488 | tf_op jit(solution)/shard_map/ppermute | solution.py:16
  308.8 2.0 collective-permute-start.19
  310.8 1.1 copy.40
  311.9 7.0 %collective-permute-done.19 = f32[1,2,288,128]{2,3,1,0:T(8,128)S(1)} collective-permute-done((f32[1,2,288,128]{2,3,1,0:T(8,128)S(1)}, f32[1,2,288,128]{2,3,1,0:T(8,128)S(1)}, u32[]{:S(2)}, u32[]{:S(2)}) %collective-permute-start.19) | collective-permute-done | bytes 294944 | tf_op jit(solution)/shard_map/ppermute | solution.py:16
  319.1 1.1 copy.41
  (78 shorter events, 7.5 us)
Async XLA Ops:
  0.6 48.7 %copy-start = (bf16[1,2,12,1152]{3,1,2,0:T(2,128)(2,1)S(1)}, bf16[1,2,12,1152]{3,1,2,0:T(2,128)(2,1)}, u32[]{:S(2)}) copy-start(bf16[1,2,12,1152]{3,1,2,0:T(2,128)(2,1)} %param.15) | copy-start | bytes 165892
  2.8 8.2 %copy-start.5 = (s32[1,2]{1,0:T(1,128)S(1)}, s32[1,2]{1,0:T(1,128)}, u32[]{:S(2)}) copy-start(s32[1,2]{1,0:T(1,128)} %param.17) | copy-start | bytes 28
  3.0 8.0 %collective-permute-start = (bf16[1,1,288,128]{2,3,1,0:T(8,128)(2,1)S(1)}, bf16[1,1,288,128]{2,3,1,0:T(8,128)(2,1)S(1)}, u32[]{:S(2)}, u32[]{:S(2)}) collective-permute-start(bf16[1,1,288,128]{2,3,1,0:T(8,128)(2,1)S(1)} %get-tuple-element.48), channel_id=1, source_target_pairs={{0,1},{1,2},{2,3},{4,5},{5,6},{6,7},{8,9},{9,10},{10,11},{12,13},{... | collective-permute-start | bytes 221192 | tf_op jit(solution)/shard_map/ppermute | solution.py:16
  7.0 6.6 %collective-permute-start.1 = (bf16[1,2,288,128]{2,3,1,0:T(8,128)(2,1)S(1)}, bf16[1,2,288,128]{2,3,1,0:T(8,128)(2,1)S(1)}, u32[]{:S(2)}, u32[]{:S(2)}) collective-permute-start(bf16[1,2,288,128]{2,3,1,0:T(8,128)(2,1)S(1)} %get-tuple-element.38), channel_id=1, source_target_pairs={{0,4},{4,8},{8,12},{12,16},{16,20},{20,24},{24,28},{1,5},{5,9},{9,... | collective-permute-start | bytes 442376 | tf_op jit(solution)/shard_map/ppermute | solution.py:16
  14.2 4.4 %copy-start.1 = (bf16[1,2,1152,1152]{3,2,1,0:T(8,128)(2,1)S(1)}, bf16[1,2,1152,1152]{3,2,1,0:T(8,128)(2,1)}, u32[]{:S(2)}) copy-start(bf16[1,2,1152,1152]{3,2,1,0:T(8,128)(2,1)} %param.13) | copy-start | bytes 15925252
  20.5 6.4 %collective-permute-start.2 = (f32[1,1,288,128]{2,3,1,0:T(8,128)S(1)}, f32[1,1,288,128]{2,3,1,0:T(8,128)S(1)}, u32[]{:S(2)}, u32[]{:S(2)}) collective-permute-start(f32[1,1,288,128]{2,3,1,0:T(8,128)S(1)} %get-tuple-element.29), channel_id=1, source_target_pairs={{1,0},{2,1},{3,2},{5,4},{6,5},{7,6},{9,8},{10,9},{11,10},{13,12},{... | collective-permute-start | bytes 442376 | tf_op jit(solution)/shard_map/ppermute | solution.py:16
  27.1 11.3 %collective-permute-start.3 = (f32[1,2,288,128]{2,3,1,0:T(8,128)S(1)}, f32[1,2,288,128]{2,3,1,0:T(8,128)S(1)}, u32[]{:S(2)}, u32[]{:S(2)}) collective-permute-start(f32[1,2,288,128]{2,3,1,0:T(8,128)S(1)} %get-tuple-element.27), channel_id=1, source_target_pairs={{4,0},{8,4},{12,8},{16,12},{20,16},{24,20},{28,24},{5,1},{9,5},{13... | collective-permute-start | bytes 884744 | tf_op jit(solution)/shard_map/ppermute | solution.py:16
  38.5 86.8 %slice-start = ((s8[5308416]{0:T(1024)(128)(4,1)}), s8[1114112]{0:T(1024)(128)(4,1)S(1)}, s32[]{:S(2)}) async-start(s8[5308416]{0:T(1024)(128)(4,1)} %bitcast.171), calls=%async_computation | async-start | bytes 2228224
  38.6 8.5 %copy-start.3 = (bf16[1,2,288,128]{2,3,1,0:T(8,128)(2,1)}, bf16[1,2,288,128]{2,3,1,0:T(8,128)(2,1)S(1)}, u32[]{:S(2)}) copy-start(bf16[1,2,288,128]{2,3,1,0:T(8,128)(2,1)S(1)} %get-tuple-element.36) | copy-start | bytes 442372
  39.3 6.0 %collective-permute-start.4 = (bf16[1,1,288,128]{2,3,1,0:T(8,128)(2,1)}, bf16[1,1,288,128]{2,3,1,0:T(8,128)(2,1)S(1)}, u32[]{:S(2)}, u32[]{:S(2)}) collective-permute-start(bf16[1,1,288,128]{2,3,1,0:T(8,128)(2,1)} %get-tuple-element.46), channel_id=1, source_target_pairs={{0,1},{1,2},{2,3},{4,5},{5,6},{6,7},{8,9},{9,10},{10,11},{12,13},{... | collective-permute-start | bytes 221192 | tf_op jit(solution)/shard_map/ppermute | solution.py:16
  42.5 4.6 %collective-permute-start.5 = (bf16[1,2,288,128]{2,3,1,0:T(8,128)(2,1)S(1)}, bf16[1,2,288,128]{2,3,1,0:T(8,128)(2,1)S(1)}, u32[]{:S(2)}, u32[]{:S(2)}) collective-permute-start(bf16[1,2,288,128]{2,3,1,0:T(8,128)(2,1)S(1)} %get-tuple-element.36), channel_id=1, source_target_pairs={{0,4},{4,8},{8,12},{12,16},{16,20},{20,24},{24,28},{1,5},{5,9},{9,... | collective-permute-start | bytes 442376 | tf_op jit(solution)/shard_map/ppermute | solution.py:16
  120.5 4.8 %slice-start.1 = ((s8[5308416]{0:T(1024)(128)(4,1)}), s8[4194304]{0:T(1024)(128)(4,1)S(1)}, s32[]{:S(2)}) async-start(s8[5308416]{0:T(1024)(128)(4,1)} %bitcast.171), calls=%async_computation.1 | async-start | bytes 8388608
  127.2 8.2 %collective-permute-start.6 = (f32[1,1,288,128]{2,3,1,0:T(8,128)S(1)}, f32[1,1,288,128]{2,3,1,0:T(8,128)S(1)}, u32[]{:S(2)}, u32[]{:S(2)}) collective-permute-start(f32[1,1,288,128]{2,3,1,0:T(8,128)S(1)} %get-tuple-element.25), channel_id=1, source_target_pairs={{1,0},{2,1},{3,2},{5,4},{6,5},{7,6},{9,8},{10,9},{11,10},{13,12},{... | collective-permute-start | bytes 442376 | tf_op jit(solution)/shard_map/ppermute | solution.py:16
  135.6 9.9 %collective-permute-start.7 = (f32[1,2,288,128]{2,3,1,0:T(8,128)S(1)}, f32[1,2,288,128]{2,3,1,0:T(8,128)S(1)}, u32[]{:S(2)}, u32[]{:S(2)}) collective-permute-start(f32[1,2,288,128]{2,3,1,0:T(8,128)S(1)} %get-tuple-element.23), channel_id=1, source_target_pairs={{4,0},{8,4},{12,8},{16,12},{20,16},{24,20},{28,24},{5,1},{9,5},{13... | collective-permute-start | bytes 884744 | tf_op jit(solution)/shard_map/ppermute | solution.py:16
  145.9 3.4 %collective-permute-start.8 = (bf16[1,1,288,128]{2,3,1,0:T(8,128)(2,1)S(1)}, bf16[1,1,288,128]{2,3,1,0:T(8,128)(2,1)S(1)}, u32[]{:S(2)}, u32[]{:S(2)}) collective-permute-start(bf16[1,1,288,128]{2,3,1,0:T(8,128)(2,1)S(1)} %get-tuple-element.44), channel_id=1, source_target_pairs={{0,1},{1,2},{2,3},{4,5},{5,6},{6,7},{8,9},{9,10},{10,11},{12,13},{... | collective-permute-start | bytes 221192 | tf_op jit(solution)/shard_map/ppermute | solution.py:16
  147.4 4.5 %collective-permute-start.9 = (bf16[1,2,288,128]{2,3,1,0:T(8,128)(2,1)S(1)}, bf16[1,2,288,128]{2,3,1,0:T(8,128)(2,1)S(1)}, u32[]{:S(2)}, u32[]{:S(2)}) collective-permute-start(bf16[1,2,288,128]{2,3,1,0:T(8,128)(2,1)S(1)} %get-tuple-element.34), channel_id=1, source_target_pairs={{0,4},{4,8},{8,12},{12,16},{16,20},{20,24},{24,28},{1,5},{5,9},{9,... | collective-permute-start | bytes 442376 | tf_op jit(solution)/shard_map/ppermute | solution.py:16
  161.1 7.9 %collective-permute-start.10 = (f32[1,1,288,128]{2,3,1,0:T(8,128)S(1)}, f32[1,1,288,128]{2,3,1,0:T(8,128)S(1)}, u32[]{:S(2)}, u32[]{:S(2)}) collective-permute-start(f32[1,1,288,128]{2,3,1,0:T(8,128)S(1)} %get-tuple-element.21), channel_id=1, source_target_pairs={{1,0},{2,1},{3,2},{5,4},{6,5},{7,6},{9,8},{10,9},{11,10},{13,12},{... | collective-permute-start | bytes 442376 | tf_op jit(solution)/shard_map/ppermute | solution.py:16
  169.2 10.3 %collective-permute-start.11 = (f32[1,2,288,128]{2,3,1,0:T(8,128)S(1)}, f32[1,2,288,128]{2,3,1,0:T(8,128)S(1)}, u32[]{:S(2)}, u32[]{:S(2)}) collective-permute-start(f32[1,2,288,128]{2,3,1,0:T(8,128)S(1)} %get-tuple-element.19), channel_id=1, source_target_pairs={{4,0},{8,4},{12,8},{16,12},{20,16},{24,20},{28,24},{5,1},{9,5},{13... | collective-permute-start | bytes 884744 | tf_op jit(solution)/shard_map/ppermute | solution.py:16
  180.8 4.5 %collective-permute-start.12 = (bf16[1,1,288,128]{2,3,1,0:T(8,128)(2,1)S(1)}, bf16[1,1,288,128]{2,3,1,0:T(8,128)(2,1)S(1)}, u32[]{:S(2)}, u32[]{:S(2)}) collective-permute-start(bf16[1,1,288,128]{2,3,1,0:T(8,128)(2,1)S(1)} %get-tuple-element.42), channel_id=1, source_target_pairs={{0,1},{1,2},{2,3},{4,5},{5,6},{6,7},{8,9},{9,10},{10,11},{12,13},{... | collective-permute-start | bytes 221192 | tf_op jit(solution)/shard_map/ppermute | solution.py:16
  183.4 4.5 %collective-permute-start.13 = (bf16[1,2,288,128]{2,3,1,0:T(8,128)(2,1)S(1)}, bf16[1,2,288,128]{2,3,1,0:T(8,128)(2,1)S(1)}, u32[]{:S(2)}, u32[]{:S(2)}) collective-permute-start(bf16[1,2,288,128]{2,3,1,0:T(8,128)(2,1)S(1)} %get-tuple-element.32), channel_id=1, source_target_pairs={{0,4},{4,8},{8,12},{12,16},{16,20},{20,24},{24,28},{1,5},{5,9},{9,... | collective-permute-start | bytes 442376 | tf_op jit(solution)/shard_map/ppermute | solution.py:16
  188.8 44.3 %copy-start.4 = (bf16[32,64]{1,0:T(8,128)(2,1)S(1)}, bf16[32,64]{1,0:T(8,128)(2,1)}, u32[]{:S(2)}) copy-start(bf16[32,64]{1,0:T(8,128)(2,1)} %param.16) | copy-start | bytes 12292
  266.7 8.2 %collective-permute-start.14 = (f32[1,1,288,128]{2,3,1,0:T(8,128)S(1)}, f32[1,1,288,128]{2,3,1,0:T(8,128)S(1)}, u32[]{:S(2)}, u32[]{:S(2)}) collective-permute-start(f32[1,1,288,128]{2,3,1,0:T(8,128)S(1)} %get-tuple-element.17), channel_id=1, source_target_pairs={{1,0},{2,1},{3,2},{5,4},{6,5},{7,6},{9,8},{10,9},{11,10},{13,12},{... | collective-permute-start | bytes 442376 | tf_op jit(solution)/shard_map/ppermute | solution.py:16
  275.0 9.9 %collective-permute-start.15 = (f32[1,2,288,128]{2,3,1,0:T(8,128)S(1)}, f32[1,2,288,128]{2,3,1,0:T(8,128)S(1)}, u32[]{:S(2)}, u32[]{:S(2)}) collective-permute-start(f32[1,2,288,128]{2,3,1,0:T(8,128)S(1)} %get-tuple-element.15), channel_id=1, source_target_pairs={{4,0},{8,4},{12,8},{16,12},{20,16},{24,20},{28,24},{5,1},{9,5},{13... | collective-permute-start | bytes 884744 | tf_op jit(solution)/shard_map/ppermute | solution.py:16
  285.4 3.4 %collective-permute-start.16 = (bf16[1,1,288,128]{2,3,1,0:T(8,128)(2,1)S(1)}, bf16[1,1,288,128]{2,3,1,0:T(8,128)(2,1)S(1)}, u32[]{:S(2)}, u32[]{:S(2)}) collective-permute-start(bf16[1,1,288,128]{2,3,1,0:T(8,128)(2,1)S(1)} %get-tuple-element.40), channel_id=1, source_target_pairs={{0,1},{1,2},{2,3},{4,5},{5,6},{6,7},{8,9},{9,10},{10,11},{12,13},{... | collective-permute-start | bytes 221192 | tf_op jit(solution)/shard_map/ppermute | solution.py:16
  286.9 4.5 %collective-permute-start.17 = (bf16[1,2,288,128]{2,3,1,0:T(8,128)(2,1)S(1)}, bf16[1,2,288,128]{2,3,1,0:T(8,128)(2,1)S(1)}, u32[]{:S(2)}, u32[]{:S(2)}) collective-permute-start(bf16[1,2,288,128]{2,3,1,0:T(8,128)(2,1)S(1)} %get-tuple-element.30), channel_id=1, source_target_pairs={{0,4},{4,8},{8,12},{12,16},{16,20},{20,24},{24,28},{1,5},{5,9},{9,... | collective-permute-start | bytes 442376 | tf_op jit(solution)/shard_map/ppermute | solution.py:16
  300.6 10.2 %copy-start.2 = (f32[1,2,2,288,128]{3,4,1,2,0:T(8,128)S(1)}, f32[1,2,2,288,128]{3,4,1,2,0:T(8,128)}, u32[]{:S(2)}) copy-start(f32[1,2,2,288,128]{3,4,1,2,0:T(8,128)} %get-tuple-element.9) | copy-start | bytes 1769476
  300.6 8.1 %collective-permute-start.18 = (f32[1,1,288,128]{2,3,1,0:T(8,128)S(1)}, f32[1,1,288,128]{2,3,1,0:T(8,128)S(1)}, u32[]{:S(2)}, u32[]{:S(2)}) collective-permute-start(f32[1,1,288,128]{2,3,1,0:T(8,128)S(1)} %get-tuple-element.13), channel_id=1, source_target_pairs={{1,0},{2,1},{3,2},{5,4},{6,5},{7,6},{9,8},{10,9},{11,10},{13,12},{... | collective-permute-start | bytes 442376 | tf_op jit(solution)/shard_map/ppermute | solution.py:16
  308.8 10.1 %collective-permute-start.19 = (f32[1,2,288,128]{2,3,1,0:T(8,128)S(1)}, f32[1,2,288,128]{2,3,1,0:T(8,128)S(1)}, u32[]{:S(2)}, u32[]{:S(2)}) collective-permute-start(f32[1,2,288,128]{2,3,1,0:T(8,128)S(1)} %get-tuple-element.11), channel_id=1, source_target_pairs={{4,0},{8,4},{12,8},{16,12},{20,16},{24,20},{28,24},{5,1},{9,5},{13... | collective-permute-start | bytes 884744 | tf_op jit(solution)/shard_map/ppermute | solution.py:16
where the time goes:
time: 321 us; the launch traced here: 320 us
  blocking collectives  138 us (43%)
  waiting for transfers between devices  81.7 us (25%)
  starting transfers between devices  42.9 us (13%)
  matrix products  40.8 us (13%)
  local copies, waits for them, and re-layouts  10.5 us (3%)
  other arithmetic  5.31 us (2%)
    ppermute x20, waiting for transfers between devices, from_behind(): return lax.ppermute(shard, axis, pairs)  81.7 us
    psum x2, blocking collectives, coarse_term(): totals = lax.psum(placed, ('sx', 'sy'))  80.9 us
    ppermute x20, starting transfers between devices, from_behind(): return lax.ppermute(shard, axis, pairs)  42.9 us
    all_gather x2, blocking collectives, coarse_term(): lax.all_gather(solved, 'sx', axis=0, tiled=True)  30.1 us
    psum x2, blocking collectives, coarse_term(): solved = lax.psum(row_part, 'sy').astype(jnp.bfloat16)  26.7 us
    dot_general x5, matrix products, paired(): jnp.einsum('rsij,rsjl->rsil', wrinkle, vectors, preferred_element_type=jn...  21.4 us
    dot_general x5, matrix products, paired(): jnp.einsum('rsij,rsjl->rsil', taut, vectors, preferred_element_type=jnp.f...  16.1 us
  transfers between devices with their start and end apart: 20, of which 15 were waited for; matrix products, arithmetic and copies ran while one was open for 1% of the time, Pallas kernels for 0%

commit v1 on v0

--- a/solution.py
+++ b/solution.py
@@ -70,7 +70,7 @@
     )
     selector_float = selector.astype(jnp.float32)
     placed = jnp.einsum("kc,kl->cl", selector_float, corner_terms, precision=lax.Precision.HIGHEST)
-    totals = lax.psum(placed, ("sx", "sy"))
+    totals = jnp.sum(lax.all_gather(placed, ("sx", "sy")), axis=0)
     column_part = lax.dynamic_slice_in_dim(totals, lax.axis_index("sy") * col_count, col_count, 0)
     row_part = jnp.dot(
         coarse_inverse, column_part.astype(jnp.bfloat16), preferred_element_type=jnp.float32

time: 321 us -> 369 us (1.15)
  waiting for transfers between devices: 81.7 us -> 196 us
  blocking collectives: 138 us -> 53.6 us
  between operations: 1.35 us -> 14.7 us
    all_gather x0 -> x2, waiting for transfers between devices: none -> 116 us  [coarse_term(): totals = jnp.sum(lax.all_gather(placed, ('sx', 'sy')), axis=0)]
    psum x2 -> x0, blocking collectives: 80.9 us -> none  [coarse_term(): totals = lax.psum(placed, ('sx', 'sy'))]
    reduce_sum x0 -> x2, other arithmetic: none -> 4.79 us  [coarse_term(): totals = jnp.sum(lax.all_gather(placed, ('sx', 'sy')), axis=0)]
    all_gather x2, blocking collectives: 30.1 us -> 26.1 us  [coarse_term(): lax.all_gather(solved, 'sx', axis=0, tiled=True)]
  transfers between devices with their start and end apart: 20 -> 22, of which waited for: 15 -> 17; matrix products, arithmetic and copies ran while one was open for 1% -> 3% of each run, Pallas kernels for 0% -> 0%
where the time goes in v1:
time: 369 us; the launch traced here: 368 us
  waiting for transfers between devices  196 us (53%)
  blocking collectives  53.6 us (15%)
  matrix products  43.7 us (12%)
  starting transfers between devices  42.8 us (12%)
  between operations  14.7 us (4%)
  other arithmetic  8.77 us (2%)
  local copies, waits for them, and re-layouts  8.3 us (2%)
    all_gather x2, waiting for transfers between devices, coarse_term(): totals = jnp.sum(lax.all_gather(placed, ('sx', 'sy')), axis=0)  116 us
    ppermute x20, waiting for transfers between devices, from_behind(): return lax.ppermute(shard, axis, pairs)  80.4 us
    ppermute x20, starting transfers between devices, from_behind(): return lax.ppermute(shard, axis, pairs)  42.7 us
    psum x2, blocking collectives, coarse_term(): solved = lax.psum(row_part, 'sy').astype(jnp.bfloat16)  27.5 us
    all_gather x2, blocking collectives, coarse_term(): lax.all_gather(solved, 'sx', axis=0, tiled=True)  26.1 us
    dot_general x5, matrix products, paired(): jnp.einsum('rsij,rsjl->rsil', wrinkle, vectors, preferred_element_type=jn...  21.1 us
    dot_general x5, matrix products, paired(): jnp.einsum('rsij,rsjl->rsil', taut, vectors, preferred_element_type=jnp.f...  18.6 us
  transfers between devices with their start and end apart: 22, of which 17 were waited for; matrix products, arithmetic and copies ran while one was open for 3% of the time, Pallas kernels for 0%

profile of v1, /device:TPU:1, one launch (start us, length us, event | category | flops | bytes accessed | tf_op | source)
XLA Modules:
  0.0 368.1 jit_solution(12246099008505629182)
XLA Ops:
  7.2 0.8 copy.32
  8.0 1.3 copy.33
  9.6 4.0 %collective-permute-start = (bf16[1,1,288,128]{2,3,1,0:T(8,128)(2,1)S(1)}, bf16[1,1,288,128]{2,3,1,0:T(8,128)(2,1)S(1)}, u32[]{:S(2)}, u32[]{:S(2)}) collective-permute-start(bf16[1,1,288,128]{2,3,1,0:T(8,128)(2,1)S(1)} %get-tuple-element.48), channel_id=1, source_target_pairs={{0,1},{1,2},{2,3},{4,5},{5,6},{6,7},{8,9},{9,10},{10,11},{12,13},{... | collective-permute-start | bytes 221192 | tf_op jit(solution)/shard_map/ppermute | solution.py:16
  13.6 4.0 %collective-permute-start.1 = (bf16[1,2,288,128]{2,3,1,0:T(8,128)(2,1)S(1)}, bf16[1,2,288,128]{2,3,1,0:T(8,128)(2,1)S(1)}, u32[]{:S(2)}, u32[]{:S(2)}) collective-permute-start(bf16[1,2,288,128]{2,3,1,0:T(8,128)(2,1)S(1)} %get-tuple-element.38), channel_id=1, source_target_pairs={{0,4},{4,8},{8,12},{12,16},{16,20},{20,24},{24,28},{1,5},{5,9},{9,... | collective-permute-start | bytes 442376 | tf_op jit(solution)/shard_map/ppermute | solution.py:16
  17.7 2.5 collective-permute-done.1
  20.2 0.6 concatenate.138
  20.8 4.3 %fusion.29 = f32[2,128,1152]{2,1,0:T(8,128)S(1)} fusion(bf16[1,2,1152,1152]{3,2,1,0:T(8,128)(2,1)} %param.14, bf16[1,2,1152,128]{2,3,1,0:T(8,128)(2,1)S(1)} %concatenate.138, f32[2]{0:T(128)S(1)} %convert_bitcast_fusion), kind=kOutput, calls=%fused_computation.23 | convolution fusion | flops 679772160 | bytes 7077896 | tf_op jit(solution)/shard_map/rsij,rsjl->rsil/dot_general | solution.py:56
  25.2 1.7 fusion.68
  27.0 1.3 collective-permute-start.2
  28.3 5.1 %collective-permute-done.2 = f32[1,1,288,128]{2,3,1,0:T(8,128)S(1)} collective-permute-done((f32[1,1,288,128]{2,3,1,0:T(8,128)S(1)}, f32[1,1,288,128]{2,3,1,0:T(8,128)S(1)}, u32[]{:S(2)}, u32[]{:S(2)}) %collective-permute-start.2) | collective-permute-done | bytes 147488 | tf_op jit(solution)/shard_map/ppermute | solution.py:16
  33.6 1.9 collective-permute-start.3
  35.6 9.3 %collective-permute-done.3 = f32[1,2,288,128]{2,3,1,0:T(8,128)S(1)} collective-permute-done((f32[1,2,288,128]{2,3,1,0:T(8,128)S(1)}, f32[1,2,288,128]{2,3,1,0:T(8,128)S(1)}, u32[]{:S(2)}, u32[]{:S(2)}) %collective-permute-start.3) | collective-permute-done | bytes 294944 | tf_op jit(solution)/shard_map/ppermute | solution.py:16
  45.3 3.2 collective-permute-start.4
  48.5 2.0 collective-permute-start.5
  50.6 2.4 collective-permute-done.5
  53.1 0.6 concatenate.141
  54.0 1.0 fusion.109
  55.1 4.2 %fusion.44 = f32[2,128,1152]{2,1,0:T(8,128)S(1)} fusion(bf16[1,2,1152,1152]{3,2,1,0:T(8,128)(2,1)} %param.12, bf16[1,2,1152,128]{2,3,1,0:T(8,128)(2,1)S(1)} %concatenate.141, f32[2]{0:T(128)S(1)} %convert_bitcast_fusion), kind=kOutput, calls=%fused_computation.28 | convolution fusion | flops 679772160 | bytes 7077896 | tf_op jit(solution)/shard_map/rsij,rsjl->rsil/dot_general | solution.py:56
  59.3 58.5 %all-gather.5.cloned.1.call-done = f32[8192,128]{1,0:T(8,128)} async-done(((f32[256,128]{1,0:T(8,128)}), f32[8192,128]{1,0:T(8,128)}) %all-gather.5.cloned.1.call-update) | async-done | bytes 4194320 | tf_op jit(solution)/shard_map/all_gather | solution.py:73
  117.8 2.4 reduce_sum.18
  120.3 13.8 %psum.14 = bf16[32,128]{1,0:T(8,128)(2,1)S(1)} all-reduce(f32[32,128]{1,0:T(8,128)S(1)} %convolution_bitcast_fusion.1), channel_id=1, replica_groups=mesh['sx'=8,'sy'=4] {'sy'}, use_global_device_ids=true, to_apply=%region_1.2 | all-reduce | flops 4096 | bytes 24576 | tf_op jit(solution)/shard_map/psum | solution.py:78
  134.1 13.1 %all_gather.20 = bf16[256,128]{1,0:T(8,128)(2,1)S(1)} all-gather(bf16[32,128]{1,0:T(8,128)(2,1)S(1)} %psum.14), channel_id=1, replica_groups=mesh['sx'=8,'sy'=4] {'sx'}, dimensions={0}, use_global_device_ids=true | all-gather | bytes 73728 | tf_op jit(solution)/shard_map/all_gather | solution.py:82
  147.7 4.2 %fusion.56 = f32[1,2,1152,128]{2,3,1,0:T(8,128)S(1)} fusion(f32[2,128,1152]{2,1,0:T(8,128)S(1)} %fusion.105, f32[2,128,1152]{2,1,0:T(8,128)S(1)} %fusion.44, bf16[1,2,1152,1152]{3,2,1,0:T(8,128)(2,1)} %param.11, bf16[1,2,1152,128]{2,3,1,0:T(8,128)(2,1)S(1)} %concatenate.141), kind=kOutput, calls=%fused_computation.32 | convolution fusion | flops 680067072 | bytes 9437184 | tf_op jit(solution)/shard_map/rsij,rsjl->rsil/dot_general | solution.py:55
  152.1 1.3 collective-permute-start.6
  153.4 6.9 %collective-permute-done.6 = f32[1,1,288,128]{2,3,1,0:T(8,128)S(1)} collective-permute-done((f32[1,1,288,128]{2,3,1,0:T(8,128)S(1)}, f32[1,1,288,128]{2,3,1,0:T(8,128)S(1)}, u32[]{:S(2)}, u32[]{:S(2)}) %collective-permute-start.6) | collective-permute-done | bytes 147488 | tf_op jit(solution)/shard_map/ppermute | solution.py:16
  160.5 2.9 collective-permute-start.7
  163.4 6.2 %collective-permute-done.7 = f32[1,2,288,128]{2,3,1,0:T(8,128)S(1)} collective-permute-done((f32[1,2,288,128]{2,3,1,0:T(8,128)S(1)}, f32[1,2,288,128]{2,3,1,0:T(8,128)S(1)}, u32[]{:S(2)}, u32[]{:S(2)}) %collective-permute-start.7) | collective-permute-done | bytes 294944 | tf_op jit(solution)/shard_map/ppermute | solution.py:16
  170.0 1.3 collective-permute-start.8
  171.3 1.9 collective-permute-start.9
  173.3 2.5 collective-permute-done.9
  175.9 0.6 concatenate.144
  176.4 4.2 %fusion.32 = f32[2,128,1152]{2,1,0:T(8,128)S(1)} fusion(bf16[1,2,1152,1152]{3,2,1,0:T(8,128)(2,1)} %param.14, bf16[1,2,1152,128]{2,3,1,0:T(8,128)(2,1)S(1)} %concatenate.144, f32[2]{0:T(128)S(1)} %convert_bitcast_fusion), kind=kOutput, calls=%fused_computation.24 | convolution fusion | flops 679772160 | bytes 7077896 | tf_op jit(solution)/shard_map/rsij,rsjl->rsil/dot_general | solution.py:56
  180.6 4.2 %fusion.65 = f32[1,2,1152,128]{2,3,1,0:T(8,128)S(1)} fusion(f32[2,128,1152]{2,1,0:T(8,128)S(1)} %fusion.32, bf16[1,2,1152,1152]{3,2,1,0:T(8,128)(2,1)} %param.13, bf16[1,2,1152,128]{2,3,1,0:T(8,128)(2,1)S(1)} %concatenate.144), kind=kOutput, calls=%fused_computation.35 | convolution fusion | flops 679772160 | bytes 8257536 | tf_op jit(solution)/shard_map/rsij,rsjl->rsil/dot_general | solution.py:55
  185.0 1.3 collective-permute-start.10
  186.3 6.6 %collective-permute-done.10 = f32[1,1,288,128]{2,3,1,0:T(8,128)S(1)} collective-permute-done((f32[1,1,288,128]{2,3,1,0:T(8,128)S(1)}, f32[1,1,288,128]{2,3,1,0:T(8,128)S(1)}, u32[]{:S(2)}, u32[]{:S(2)}) %collective-permute-start.10) | collective-permute-done | bytes 147488 | tf_op jit(solution)/shard_map/ppermute | solution.py:16
  193.1 2.2 collective-permute-start.11
  195.3 7.5 %collective-permute-done.11 = f32[1,2,288,128]{2,3,1,0:T(8,128)S(1)} collective-permute-done((f32[1,2,288,128]{2,3,1,0:T(8,128)S(1)}, f32[1,2,288,128]{2,3,1,0:T(8,128)S(1)}, u32[]{:S(2)}, u32[]{:S(2)}) %collective-permute-start.11) | collective-permute-done | bytes 294944 | tf_op jit(solution)/shard_map/ppermute | solution.py:16
  203.0 1.2 fusion.117
  204.2 2.6 collective-permute-start.12
  206.8 1.9 collective-permute-start.13
  208.8 2.5 collective-permute-done.13
  212.2 1.0 fusion.108
  213.2 4.2 %fusion.47 = f32[2,128,1152]{2,1,0:T(8,128)S(1)} fusion(bf16[1,2,1152,1152]{3,2,1,0:T(8,128)(2,1)} %param.12, bf16[1,2,1152,128]{2,3,1,0:T(8,128)(2,1)S(1)} %concatenate.147, f32[2]{0:T(128)S(1)} %convert_bitcast_fusion), kind=kOutput, calls=%fused_computation.29 | convolution fusion | flops 679772160 | bytes 7077896 | tf_op jit(solution)/shard_map/rsij,rsjl->rsil/dot_general | solution.py:56
  217.4 57.3 %all-gather.7.cloned.1.call-done = f32[8192,128]{1,0:T(8,128)} async-done(((f32[256,128]{1,0:T(8,128)}), f32[8192,128]{1,0:T(8,128)}) %all-gather.7.cloned.1.call-update) | async-done | bytes 4194320 | tf_op jit(solution)/shard_map/all_gather | solution.py:73
  274.8 2.4 reduce_sum.19
  277.3 13.8 %psum.15 = bf16[32,128]{1,0:T(8,128)(2,1)S(1)} all-reduce(f32[32,128]{1,0:T(8,128)S(1)} %convolution_bitcast_fusion), channel_id=1, replica_groups=mesh['sx'=8,'sy'=4] {'sy'}, use_global_device_ids=true, to_apply=%region_3.4 | all-reduce | flops 4096 | bytes 24576 | tf_op jit(solution)/shard_map/psum | solution.py:78
  291.1 13.1 %all_gather.23 = bf16[256,128]{1,0:T(8,128)(2,1)S(1)} all-gather(bf16[32,128]{1,0:T(8,128)(2,1)S(1)} %psum.15), channel_id=1, replica_groups=mesh['sx'=8,'sy'=4] {'sx'}, dimensions={0}, use_global_device_ids=true | all-gather | bytes 73728 | tf_op jit(solution)/shard_map/all_gather | solution.py:82
  304.7 4.2 %fusion.59 = f32[1,2,1152,128]{2,3,1,0:T(8,128)S(1)} fusion(f32[2,128,1152]{2,1,0:T(8,128)S(1)} %fusion.102, f32[2,128,1152]{2,1,0:T(8,128)S(1)} %fusion.47, bf16[1,2,1152,1152]{3,2,1,0:T(8,128)(2,1)} %param.11, bf16[1,2,1152,128]{2,3,1,0:T(8,128)(2,1)S(1)} %concatenate.147), kind=kOutput, calls=%fused_computation.33 | convolution fusion | flops 680067072 | bytes 9437184 | tf_op jit(solution)/shard_map/rsij,rsjl->rsil/dot_general | solution.py:55
  309.1 1.3 collective-permute-start.14
  310.4 6.9 %collective-permute-done.14 = f32[1,1,288,128]{2,3,1,0:T(8,128)S(1)} collective-permute-done((f32[1,1,288,128]{2,3,1,0:T(8,128)S(1)}, f32[1,1,288,128]{2,3,1,0:T(8,128)S(1)}, u32[]{:S(2)}, u32[]{:S(2)}) %collective-permute-start.14) | collective-permute-done | bytes 147488 | tf_op jit(solution)/shard_map/ppermute | solution.py:16
  317.5 2.9 collective-permute-start.15
  320.4 6.2 %collective-permute-done.15 = f32[1,2,288,128]{2,3,1,0:T(8,128)S(1)} collective-permute-done((f32[1,2,288,128]{2,3,1,0:T(8,128)S(1)}, f32[1,2,288,128]{2,3,1,0:T(8,128)S(1)}, u32[]{:S(2)}, u32[]{:S(2)}) %collective-permute-start.15) | collective-permute-done | bytes 294944 | tf_op jit(solution)/shard_map/ppermute | solution.py:16
  327.0 1.3 collective-permute-start.16
  328.3 1.9 collective-permute-start.17
  330.3 2.5 collective-permute-done.17
  332.8 0.6 concatenate.150
  333.4 4.2 %fusion.35 = f32[2,128,1152]{2,1,0:T(8,128)S(1)} fusion(bf16[1,2,1152,1152]{3,2,1,0:T(8,128)(2,1)} %param.14, bf16[1,2,1152,128]{2,3,1,0:T(8,128)(2,1)S(1)} %concatenate.150, f32[2]{0:T(128)S(1)} %convert_bitcast_fusion), kind=kOutput, calls=%fused_computation.25 | convolution fusion | flops 679772160 | bytes 7077896 | tf_op jit(solution)/shard_map/rsij,rsjl->rsil/dot_general | solution.py:56
  337.6 4.2 %fusion.62 = f32[1,2,1152,128]{2,3,1,0:T(8,128)S(1)} fusion(f32[2,128,1152]{2,1,0:T(8,128)S(1)} %fusion.35, bf16[1,2,1152,1152]{3,2,1,0:T(8,128)(2,1)} %param.13, bf16[1,2,1152,128]{2,3,1,0:T(8,128)(2,1)S(1)} %concatenate.150), kind=kOutput, calls=%fused_computation.34 | convolution fusion | flops 679772160 | bytes 8257536 | tf_op jit(solution)/shard_map/rsij,rsjl->rsil/dot_general | solution.py:55
  342.0 1.4 collective-permute-start.18
  343.4 6.6 %collective-permute-done.18 = f32[1,1,288,128]{2,3,1,0:T(8,128)S(1)} collective-permute-done((f32[1,1,288,128]{2,3,1,0:T(8,128)S(1)}, f32[1,1,288,128]{2,3,1,0:T(8,128)S(1)}, u32[]{:S(2)}, u32[]{:S(2)}) %collective-permute-start.18) | collective-permute-done | bytes 147488 | tf_op jit(solution)/shard_map/ppermute | solution.py:16
  350.2 2.0 collective-permute-start.19
  352.2 1.1 copy.40
  353.3 6.6 %collective-permute-done.19 = f32[1,2,288,128]{2,3,1,0:T(8,128)S(1)} collective-permute-done((f32[1,2,288,128]{2,3,1,0:T(8,128)S(1)}, f32[1,2,288,128]{2,3,1,0:T(8,128)S(1)}, u32[]{:S(2)}, u32[]{:S(2)}) %collective-permute-start.19) | collective-permute-done | bytes 294944 | tf_op jit(solution)/shard_map/ppermute | solution.py:16
  360.2 1.1 copy.41
  (79 shorter events, 6.7 us)
Async XLA Ops:
  7.2 46.5 %copy-start = (bf16[1,2,12,1152]{3,1,2,0:T(2,128)(2,1)S(1)}, bf16[1,2,12,1152]{3,1,2,0:T(2,128)(2,1)}, u32[]{:S(2)}) copy-start(bf16[1,2,12,1152]{3,1,2,0:T(2,128)(2,1)} %param.15) | copy-start | bytes 165892
  7.2 110.6 %all-gather.5.cloned.1.call-start = ((), (), s32[]{:S(2)}) async-start(), calls=%async_computation | async-start | bytes 4325376 | tf_op jit(solution)/shard_map/all_gather | solution.py:73
  9.4 8.2 %copy-start.5 = (s32[1,2]{1,0:T(1,128)S(1)}, s32[1,2]{1,0:T(1,128)}, u32[]{:S(2)}) copy-start(s32[1,2]{1,0:T(1,128)} %param.17) | copy-start | bytes 28
  9.6 8.0 %collective-permute-start = (bf16[1,1,288,128]{2,3,1,0:T(8,128)(2,1)S(1)}, bf16[1,1,288,128]{2,3,1,0:T(8,128)(2,1)S(1)}, u32[]{:S(2)}, u32[]{:S(2)}) collective-permute-start(bf16[1,1,288,128]{2,3,1,0:T(8,128)(2,1)S(1)} %get-tuple-element.48), channel_id=1, source_target_pairs={{0,1},{1,2},{2,3},{4,5},{5,6},{6,7},{8,9},{9,10},{10,11},{12,13},{... | collective-permute-start | bytes 221192 | tf_op jit(solution)/shard_map/ppermute | solution.py:16
  13.6 6.6 %collective-permute-start.1 = (bf16[1,2,288,128]{2,3,1,0:T(8,128)(2,1)S(1)}, bf16[1,2,288,128]{2,3,1,0:T(8,128)(2,1)S(1)}, u32[]{:S(2)}, u32[]{:S(2)}) collective-permute-start(bf16[1,2,288,128]{2,3,1,0:T(8,128)(2,1)S(1)} %get-tuple-element.38), channel_id=1, source_target_pairs={{0,4},{4,8},{8,12},{12,16},{16,20},{20,24},{24,28},{1,5},{5,9},{9,... | collective-permute-start | bytes 442376 | tf_op jit(solution)/shard_map/ppermute | solution.py:16
  20.8 4.4 %copy-start.1 = (bf16[1,2,1152,1152]{3,2,1,0:T(8,128)(2,1)S(1)}, bf16[1,2,1152,1152]{3,2,1,0:T(8,128)(2,1)}, u32[]{:S(2)}) copy-start(bf16[1,2,1152,1152]{3,2,1,0:T(8,128)(2,1)} %param.13) | copy-start | bytes 15925252
  27.0 6.4 %collective-permute-start.2 = (f32[1,1,288,128]{2,3,1,0:T(8,128)S(1)}, f32[1,1,288,128]{2,3,1,0:T(8,128)S(1)}, u32[]{:S(2)}, u32[]{:S(2)}) collective-permute-start(f32[1,1,288,128]{2,3,1,0:T(8,128)S(1)} %get-tuple-element.29), channel_id=1, source_target_pairs={{1,0},{2,1},{3,2},{5,4},{6,5},{7,6},{9,8},{10,9},{11,10},{13,12},{... | collective-permute-start | bytes 442376 | tf_op jit(solution)/shard_map/ppermute | solution.py:16
  33.6 11.3 %collective-permute-start.3 = (f32[1,2,288,128]{2,3,1,0:T(8,128)S(1)}, f32[1,2,288,128]{2,3,1,0:T(8,128)S(1)}, u32[]{:S(2)}, u32[]{:S(2)}) collective-permute-start(f32[1,2,288,128]{2,3,1,0:T(8,128)S(1)} %get-tuple-element.27), channel_id=1, source_target_pairs={{4,0},{8,4},{12,8},{16,12},{20,16},{24,20},{28,24},{5,1},{9,5},{13... | collective-permute-start | bytes 884744 | tf_op jit(solution)/shard_map/ppermute | solution.py:16
  45.1 5.4 %copy-start.4 = (s32[1,2,12]{2,1,0:T(2,128)S(1)}, s32[1,2,12]{2,1,0:T(2,128)}, u32[]{:S(2)}) copy-start(s32[1,2,12]{2,1,0:T(2,128)} %param.19) | copy-start | bytes 292
  45.3 5.3 %collective-permute-start.4 = (bf16[1,1,288,128]{2,3,1,0:T(8,128)(2,1)S(1)}, bf16[1,1,288,128]{2,3,1,0:T(8,128)(2,1)S(1)}, u32[]{:S(2)}, u32[]{:S(2)}) collective-permute-start(bf16[1,1,288,128]{2,3,1,0:T(8,128)(2,1)S(1)} %get-tuple-element.46), channel_id=1, source_target_pairs={{0,1},{1,2},{2,3},{4,5},{5,6},{6,7},{8,9},{9,10},{10,11},{12,13},{... | collective-permute-start | bytes 221192 | tf_op jit(solution)/shard_map/ppermute | solution.py:16
  48.5 4.6 %collective-permute-start.5 = (bf16[1,2,288,128]{2,3,1,0:T(8,128)(2,1)S(1)}, bf16[1,2,288,128]{2,3,1,0:T(8,128)(2,1)S(1)}, u32[]{:S(2)}, u32[]{:S(2)}) collective-permute-start(bf16[1,2,288,128]{2,3,1,0:T(8,128)(2,1)S(1)} %get-tuple-element.36), channel_id=1, source_target_pairs={{0,4},{4,8},{8,12},{12,16},{16,20},{20,24},{24,28},{1,5},{5,9},{9,... | collective-permute-start | bytes 442376 | tf_op jit(solution)/shard_map/ppermute | solution.py:16
  55.0 219.7 %all-gather.7.cloned.1.call-start = ((), (), s32[]{:S(2)}) async-start(), calls=%async_computation.1 | async-start | bytes 4325376 | tf_op jit(solution)/shard_map/all_gather | solution.py:73
  117.8 2.4 copy-start.3
  152.1 8.2 %collective-permute-start.6 = (f32[1,1,288,128]{2,3,1,0:T(8,128)S(1)}, f32[1,1,288,128]{2,3,1,0:T(8,128)S(1)}, u32[]{:S(2)}, u32[]{:S(2)}) collective-permute-start(f32[1,1,288,128]{2,3,1,0:T(8,128)S(1)} %get-tuple-element.25), channel_id=1, source_target_pairs={{1,0},{2,1},{3,2},{5,4},{6,5},{7,6},{9,8},{10,9},{11,10},{13,12},{... | collective-permute-start | bytes 442376 | tf_op jit(solution)/shard_map/ppermute | solution.py:16
  160.5 9.1 %collective-permute-start.7 = (f32[1,2,288,128]{2,3,1,0:T(8,128)S(1)}, f32[1,2,288,128]{2,3,1,0:T(8,128)S(1)}, u32[]{:S(2)}, u32[]{:S(2)}) collective-permute-start(f32[1,2,288,128]{2,3,1,0:T(8,128)S(1)} %get-tuple-element.23), channel_id=1, source_target_pairs={{4,0},{8,4},{12,8},{16,12},{20,16},{24,20},{28,24},{5,1},{9,5},{13... | collective-permute-start | bytes 884744 | tf_op jit(solution)/shard_map/ppermute | solution.py:16
  170.0 3.2 collective-permute-start.8
  171.3 4.5 %collective-permute-start.9 = (bf16[1,2,288,128]{2,3,1,0:T(8,128)(2,1)S(1)}, bf16[1,2,288,128]{2,3,1,0:T(8,128)(2,1)S(1)}, u32[]{:S(2)}, u32[]{:S(2)}) collective-permute-start(bf16[1,2,288,128]{2,3,1,0:T(8,128)(2,1)S(1)} %get-tuple-element.34), channel_id=1, source_target_pairs={{0,4},{4,8},{8,12},{12,16},{16,20},{20,24},{24,28},{1,5},{5,9},{9,... | collective-permute-start | bytes 442376 | tf_op jit(solution)/shard_map/ppermute | solution.py:16
  185.0 7.9 %collective-permute-start.10 = (f32[1,1,288,128]{2,3,1,0:T(8,128)S(1)}, f32[1,1,288,128]{2,3,1,0:T(8,128)S(1)}, u32[]{:S(2)}, u32[]{:S(2)}) collective-permute-start(f32[1,1,288,128]{2,3,1,0:T(8,128)S(1)} %get-tuple-element.21), channel_id=1, source_target_pairs={{1,0},{2,1},{3,2},{5,4},{6,5},{7,6},{9,8},{10,9},{11,10},{13,12},{... | collective-permute-start | bytes 442376 | tf_op jit(solution)/shard_map/ppermute | solution.py:16
  193.1 9.7 %collective-permute-start.11 = (f32[1,2,288,128]{2,3,1,0:T(8,128)S(1)}, f32[1,2,288,128]{2,3,1,0:T(8,128)S(1)}, u32[]{:S(2)}, u32[]{:S(2)}) collective-permute-start(f32[1,2,288,128]{2,3,1,0:T(8,128)S(1)} %get-tuple-element.19), channel_id=1, source_target_pairs={{4,0},{8,4},{12,8},{16,12},{20,16},{24,20},{28,24},{5,1},{9,5},{13... | collective-permute-start | bytes 884744 | tf_op jit(solution)/shard_map/ppermute | solution.py:16
  204.2 4.5 %collective-permute-start.12 = (bf16[1,1,288,128]{2,3,1,0:T(8,128)(2,1)S(1)}, bf16[1,1,288,128]{2,3,1,0:T(8,128)(2,1)S(1)}, u32[]{:S(2)}, u32[]{:S(2)}) collective-permute-start(bf16[1,1,288,128]{2,3,1,0:T(8,128)(2,1)S(1)} %get-tuple-element.42), channel_id=1, source_target_pairs={{0,1},{1,2},{2,3},{4,5},{5,6},{6,7},{8,9},{9,10},{10,11},{12,13},{... | collective-permute-start | bytes 221192 | tf_op jit(solution)/shard_map/ppermute | solution.py:16
  206.8 4.5 %collective-permute-start.13 = (bf16[1,2,288,128]{2,3,1,0:T(8,128)(2,1)S(1)}, bf16[1,2,288,128]{2,3,1,0:T(8,128)(2,1)S(1)}, u32[]{:S(2)}, u32[]{:S(2)}) collective-permute-start(bf16[1,2,288,128]{2,3,1,0:T(8,128)(2,1)S(1)} %get-tuple-element.32), channel_id=1, source_target_pairs={{0,4},{4,8},{8,12},{12,16},{16,20},{20,24},{24,28},{1,5},{5,9},{9,... | collective-permute-start | bytes 442376 | tf_op jit(solution)/shard_map/ppermute | solution.py:16
  309.1 8.2 %collective-permute-start.14 = (f32[1,1,288,128]{2,3,1,0:T(8,128)S(1)}, f32[1,1,288,128]{2,3,1,0:T(8,128)S(1)}, u32[]{:S(2)}, u32[]{:S(2)}) collective-permute-start(f32[1,1,288,128]{2,3,1,0:T(8,128)S(1)} %get-tuple-element.17), channel_id=1, source_target_pairs={{1,0},{2,1},{3,2},{5,4},{6,5},{7,6},{9,8},{10,9},{11,10},{13,12},{... | collective-permute-start | bytes 442376 | tf_op jit(solution)/shard_map/ppermute | solution.py:16
  317.5 9.1 %collective-permute-start.15 = (f32[1,2,288,128]{2,3,1,0:T(8,128)S(1)}, f32[1,2,288,128]{2,3,1,0:T(8,128)S(1)}, u32[]{:S(2)}, u32[]{:S(2)}) collective-permute-start(f32[1,2,288,128]{2,3,1,0:T(8,128)S(1)} %get-tuple-element.15), channel_id=1, source_target_pairs={{4,0},{8,4},{12,8},{16,12},{20,16},{24,20},{28,24},{5,1},{9,5},{13... | collective-permute-start | bytes 884744 | tf_op jit(solution)/shard_map/ppermute | solution.py:16
  327.0 3.2 collective-permute-start.16
  328.3 4.5 %collective-permute-start.17 = (bf16[1,2,288,128]{2,3,1,0:T(8,128)(2,1)S(1)}, bf16[1,2,288,128]{2,3,1,0:T(8,128)(2,1)S(1)}, u32[]{:S(2)}, u32[]{:S(2)}) collective-permute-start(bf16[1,2,288,128]{2,3,1,0:T(8,128)(2,1)S(1)} %get-tuple-element.30), channel_id=1, source_target_pairs={{0,4},{4,8},{8,12},{12,16},{16,20},{20,24},{24,28},{1,5},{5,9},{9,... | collective-permute-start | bytes 442376 | tf_op jit(solution)/shard_map/ppermute | solution.py:16
  342.0 10.2 %copy-start.2 = (f32[1,2,2,288,128]{3,4,1,2,0:T(8,128)S(1)}, f32[1,2,2,288,128]{3,4,1,2,0:T(8,128)}, u32[]{:S(2)}) copy-start(f32[1,2,2,288,128]{3,4,1,2,0:T(8,128)} %get-tuple-element.9) | copy-start | bytes 1769476
  342.0 8.1 %collective-permute-start.18 = (f32[1,1,288,128]{2,3,1,0:T(8,128)S(1)}, f32[1,1,288,128]{2,3,1,0:T(8,128)S(1)}, u32[]{:S(2)}, u32[]{:S(2)}) collective-permute-start(f32[1,1,288,128]{2,3,1,0:T(8,128)S(1)} %get-tuple-element.13), channel_id=1, source_target_pairs={{1,0},{2,1},{3,2},{5,4},{6,5},{7,6},{9,8},{10,9},{11,10},{13,12},{... | collective-permute-start | bytes 442376 | tf_op jit(solution)/shard_map/ppermute | solution.py:16
  350.2 9.7 %collective-permute-start.19 = (f32[1,2,288,128]{2,3,1,0:T(8,128)S(1)}, f32[1,2,288,128]{2,3,1,0:T(8,128)S(1)}, u32[]{:S(2)}, u32[]{:S(2)}) collective-permute-start(f32[1,2,288,128]{2,3,1,0:T(8,128)S(1)} %get-tuple-element.11), channel_id=1, source_target_pairs={{4,0},{8,4},{12,8},{16,12},{20,16},{24,20},{28,24},{5,1},{9,5},{13... | collective-permute-start | bytes 884744 | tf_op jit(solution)/shard_map/ppermute | solution.py:16
Sparse Core Ops, SparseCore 0:
  55.2 62.5 all-gather.4
  213.4 61.3 all-gather.6
